TPU v7x, 32 devices: a whole 2x2x4 slice. The times are simulated.
32 devices in a mesh: row: 8 (over z, y), col: 4 (over x, core).
Axes of the slice: x: 2, y: 2, z: 4, core: 2. Of those that a mesh axis runs over, the one named last changes fastest.
Arguments:
- tokens: bfloat16 [1600, 8192], P('row', 'col')
- ln1_gain: float32 [1600], P('row'), may hold values from 0.25 to 1.75
- ln1_shift: float32 [1600], P('row'), may hold values from -4 to 4
- weight_qkv: bfloat16 [1600, 4800], P('row', 'col'), may hold values from -0.21875 to 0.21875
- bias_qkv: float32 [4800], P('col'), may hold values from -4 to 4
- weight_out: bfloat16 [1600, 1600], P('row', 'col'), may hold values from -0.625 to 0.625
- bias_out: float32 [1600], P('row'), may hold values from -6 to 6
- ln2_gain: float32 [1600], P('row'), may hold values from 0.25 to 1.75
- ln2_shift: float32 [1600], P('row'), may hold values from -4 to 4
- weight_up: bfloat16 [1600, 6400], P('row', 'col'), may hold values from -0.15625 to 0.15625
- bias_up: float32 [6400], P('col'), may hold values from -6 to 6
- weight_down: bfloat16 [1600, 6400], P('row', 'col'), may hold values from -0.109375 to 0.109375
- bias_down: float32 [1600], P('row'), may hold values from -6 to 6
- cotangent: bfloat16 [1600, 8192], P('row', 'col')
Outputs:
- block_output: bfloat16 [1600, 8192], P('row', 'col')
- grad_tokens: float32 [1600, 8192], P('row', 'col')
- grad_ln1_gain: float32 [1600], P('row')
- grad_ln1_shift: float32 [1600], P('row')
- grad_weight_qkv: float32 [1600, 4800], P('row', 'col')
- grad_bias_qkv: float32 [4800], P('col')
- grad_weight_out: float32 [1600, 1600], P('row', 'col')
- grad_bias_out: float32 [1600], P('row')
- grad_ln2_gain: float32 [1600], P('row')
- grad_ln2_shift: float32 [1600], P('row')
- grad_weight_up: float32 [1600, 6400], P('row', 'col')
- grad_bias_up: float32 [6400], P('col')
- grad_weight_down: float32 [1600, 6400], P('row', 'col')
- grad_bias_down: float32 [1600], P('row')
All inputs are finite; a program needn't handle non-finite values.
Results may differ from a plain program's by a relative error of at most 0.012.
The roundings to bfloat16 on the way count: a program that leaves them out, or rounds other values in their place, can miss the bound.
Values may be sent and summed in bfloat16 or wider, within the bound.
A program may use at most 256 MiB of HBM per device.

v0:
```python
import jax
import jax.numpy as jnp
from jax import lax
from jax.sharding import PartitionSpec as P

D = 1600
H = 25
HD = 64
L = 1024
SEQ_ROW = 1
epsilon = 1e-05
excluded = -1e30


def row_totals(first_sum, second_sum):
    return lax.psum((first_sum, second_sum), "row")


def norm_forward(values, norm_gain, norm_shift):
    row_sum, row_squares = row_totals(jnp.sum(values, axis=0), jnp.sum(values * values, axis=0))
    row_mean = row_sum / D
    row_scale = lax.rsqrt(row_squares / D - row_mean * row_mean + epsilon)
    centred = (values - row_mean[None, :]) * row_scale[None, :]
    return (
        (centred * norm_gain[:, None] + norm_shift[:, None]).astype(jnp.bfloat16),
        centred,
        row_scale,
    )


def norm_backward(gradient, centred, row_scale, norm_gain):
    scaled = gradient * norm_gain[:, None]
    first_sum, second_sum = row_totals(jnp.sum(scaled, axis=0), jnp.sum(scaled * centred, axis=0))
    adjusted = scaled - first_sum[None, :] / D - centred * (second_sum[None, :] / D)
    return (
        adjusted * row_scale[None, :],
        jnp.sum(gradient * centred, axis=1),
        jnp.sum(gradient, axis=1),
    )


def spread_cols(values):
    return lax.all_gather(values, "col", axis=1, tiled=True)


def row_terms(gathered, weight):
    return lax.psum_scatter(
        lax.dot_general(
            gathered, weight, (((0,), (0,)), ((), ())), preferred_element_type=jnp.float32
        ),
        "row",
        scatter_dimension=0,
        tiled=True,
    )


def project_rows(gathered, weight):
    return row_terms(gathered, weight)


def share_cols(full_cols):
    return lax.psum_scatter(full_cols, "col", scatter_dimension=1, tiled=True)


def cross_products(values, weight):
    return share_cols(
        lax.dot_general(
            weight,
            lax.all_gather(values, "row", axis=0, tiled=True),
            (((1,), (1,)), ((), ())),
            preferred_element_type=jnp.float32,
        )
    )


def fold_rows(gradient, weight, gathered):

    def accumulate(running, block_rows, offset):
        through = lax.dot_general(
            weight, block_rows, (((1,), (1,)), ((), ())), preferred_element_type=jnp.float32
        )
        weight_grad = jnp.dot(gathered, block_rows, preferred_element_type=jnp.float32)
        return (through, weight_grad)

    initial = (
        jnp.zeros((weight.shape[0], gathered.shape[1]), jnp.float32),
        jnp.zeros(weight.shape, jnp.float32),
    )
    return accumulate(initial, lax.all_gather(gradient, "row", axis=0, tiled=True), jnp.int32(0))


def fold_again(values, gathered):

    def accumulate(running, block_rows, offset):
        return jnp.dot(gathered, block_rows, preferred_element_type=jnp.float32)

    initial = jnp.zeros((gathered.shape[0], values.shape[1]), jnp.float32)
    return accumulate(initial, lax.all_gather(values, "row", axis=0, tiled=True), jnp.int32(0))


def build_slots():
    col_count = lax.axis_size("col")
    unit_count = SEQ_ROW * H
    slot_count = (unit_count + col_count - 1) // col_count
    column_ids = jnp.arange(col_count, dtype=jnp.int32)[:, None]
    slot_ids = jnp.arange(slot_count, dtype=jnp.int32)[None, :]
    numbered = slot_ids * col_count + column_ids
    return jnp.where(numbered < unit_count, numbered, -1)


def slot_matrix(slot_table):
    return (
        slot_table.reshape(-1)[:, None] == jnp.arange(SEQ_ROW * H, dtype=jnp.int32)[None, :]
    ).astype(jnp.bfloat16)


def to_units(values, slot_table):
    channels = values.shape[1] // H
    by_unit = (
        values.reshape(SEQ_ROW, L, channels, H)
        .transpose(0, 3, 1, 2)
        .reshape(SEQ_ROW * H, L * channels)
    )
    outgoing = jnp.dot(slot_matrix(slot_table), by_unit, preferred_element_type=jnp.float32).astype(
        jnp.bfloat16
    )
    outgoing = outgoing.reshape(slot_table.shape[0], slot_table.shape[1], L, channels)
    return lax.all_to_all(outgoing, "col", split_axis=0, concat_axis=3, tiled=True)[0]


def to_tokens(unit_values, slot_table):
    returned = lax.all_to_all(unit_values[None], "col", split_axis=3, concat_axis=0, tiled=True)
    channels = returned.shape[3]
    flat = returned.reshape(slot_table.shape[0] * slot_table.shape[1], L * channels)
    placed = lax.dot_general(
        slot_matrix(slot_table), flat, (((0,), (0,)), ((), ())), preferred_element_type=jnp.float32
    )
    placed = placed.astype(jnp.bfloat16).reshape(SEQ_ROW, H, L, channels)
    return placed.transpose(0, 2, 3, 1).reshape(SEQ_ROW * L, channels * H)


def causal_mask():
    return jnp.arange(L)[:, None] >= jnp.arange(L)[None, :]


def attend_forward(unit_data):
    score_scale = HD ** (-0.5)
    allowed = causal_mask()

    def per_unit(unit_rows):
        query_rows = unit_rows[:, :HD]
        key_rows = unit_rows[:, HD : 2 * HD]
        value_rows = unit_rows[:, 2 * HD :]
        scores = (
            lax.dot_general(
                query_rows, key_rows, (((1,), (1,)), ((), ())), preferred_element_type=jnp.float32
            )
            * score_scale
        )
        scores = jnp.where(allowed, scores, excluded)
        peak = jnp.max(scores, axis=1, keepdims=True)
        weights = jnp.exp(scores - peak)
        row_total = jnp.sum(weights, axis=1, keepdims=True)
        weights_low = (weights / row_total).astype(jnp.bfloat16)
        attended = jnp.dot(weights_low, value_rows, preferred_element_type=jnp.float32).astype(
            jnp.bfloat16
        )
        return (attended, (peak + jnp.log(row_total))[:, 0])

    return lax.map(per_unit, unit_data)


def attend_backward(unit_data, grad_units, log_totals):
    score_scale = HD ** (-0.5)
    allowed = causal_mask()

    def per_unit(inputs):
        unit_rows, grad_rows, log_row = inputs
        query_rows = unit_rows[:, :HD]
        key_rows = unit_rows[:, HD : 2 * HD]
        value_rows = unit_rows[:, 2 * HD :]
        scores = (
            lax.dot_general(
                query_rows, key_rows, (((1,), (1,)), ((), ())), preferred_element_type=jnp.float32
            )
            * score_scale
        )
        scores = jnp.where(allowed, scores, excluded)
        weights = jnp.exp(scores - log_row[:, None])
        weights_low = weights.astype(jnp.bfloat16)
        grad_value = lax.dot_general(
            weights_low, grad_rows, (((0,), (0,)), ((), ())), preferred_element_type=jnp.float32
        )
        grad_weights = lax.dot_general(
            grad_rows, value_rows, (((1,), (1,)), ((), ())), preferred_element_type=jnp.float32
        )
        grad_scores = weights * (
            grad_weights - jnp.sum(weights * grad_weights, axis=1, keepdims=True)
        )
        grad_low = grad_scores.astype(jnp.bfloat16)
        grad_query = jnp.dot(grad_low, key_rows, preferred_element_type=jnp.float32) * score_scale
        grad_key = (
            lax.dot_general(
                grad_low, query_rows, (((0,), (0,)), ((), ())), preferred_element_type=jnp.float32
            )
            * score_scale
        )
        return jnp.concatenate([grad_query, grad_key, grad_value], axis=1).astype(jnp.bfloat16)

    return lax.map(per_unit, (unit_data, grad_units, log_totals))


def body(
    tokens,
    ln1_gain,
    ln1_shift,
    weight_qkv,
    bias_qkv,
    weight_out,
    bias_out,
    ln2_gain,
    ln2_shift,
    weight_up,
    bias_up,
    weight_down,
    bias_down,
    cotangent,
):
    slot_table = build_slots()
    residual_in = tokens.astype(jnp.float32)
    normed_in, centred_in, scale_in = norm_forward(residual_in, ln1_gain, ln1_shift)
    normed_wide = spread_cols(normed_in)
    qkv_rows = (project_rows(normed_wide, weight_qkv) + bias_qkv).astype(jnp.bfloat16)
    unit_data = to_units(qkv_rows, slot_table)
    attended_units, log_totals = attend_forward(unit_data)
    attended_rows = to_tokens(attended_units, slot_table)
    residual_mid = residual_in + cross_products(attended_rows, weight_out) + bias_out[:, None]
    normed_mid, centred_mid, scale_mid = norm_forward(residual_mid, ln2_gain, ln2_shift)
    mid_wide = spread_cols(normed_mid)
    hidden_pre = project_rows(mid_wide, weight_up) + bias_up
    hidden_rows = jax.nn.gelu(hidden_pre, approximate=True).astype(jnp.bfloat16)
    block_output = (
        residual_mid + cross_products(hidden_rows, weight_down) + bias_down[:, None]
    ).astype(jnp.bfloat16)
    grad_wide = spread_cols(cotangent)
    grad_bias_down = jnp.sum(grad_wide, axis=1, dtype=jnp.float32)
    grad_hidden = project_rows(grad_wide, weight_down)
    unused_value, gelu_back = jax.vjp(
        lambda inner: jax.nn.gelu(inner, approximate=True), hidden_pre
    )
    grad_pre = gelu_back(grad_hidden)[0].astype(jnp.bfloat16)
    up_part = jnp.sum(grad_pre, axis=0, dtype=jnp.float32)
    mid_full, grad_weight_up = fold_rows(grad_pre, weight_up, mid_wide)
    grad_normed_mid = share_cols(mid_full)
    grad_norm_mid, gain_two_part, shift_two_part = norm_backward(
        grad_normed_mid, centred_mid, scale_mid, ln2_gain
    )
    grad_residual_mid = cotangent.astype(jnp.float32) + grad_norm_mid
    grad_branch = grad_residual_mid.astype(jnp.bfloat16)
    branch_wide = spread_cols(grad_branch)
    grad_bias_out = jnp.sum(branch_wide, axis=1, dtype=jnp.float32)
    grad_attended = project_rows(branch_wide, weight_out).astype(jnp.bfloat16)
    grad_units = to_units(grad_attended, slot_table)
    grad_unit_qkv = attend_backward(unit_data, grad_units, log_totals)
    grad_qkv_rows = to_tokens(grad_unit_qkv, slot_table)
    qkv_part = jnp.sum(grad_qkv_rows, axis=0, dtype=jnp.float32)
    in_full, grad_weight_qkv = fold_rows(grad_qkv_rows, weight_qkv, normed_wide)
    grad_normed_in = share_cols(in_full)
    grad_norm_in, gain_one_part, shift_one_part = norm_backward(
        grad_normed_in, centred_in, scale_in, ln1_gain
    )
    grad_tokens = grad_residual_mid + grad_norm_in
    grad_weight_down = fold_again(hidden_rows, grad_wide)
    grad_weight_out = fold_again(attended_rows, branch_wide)
    grad_bias_up, grad_bias_qkv = lax.psum((up_part, qkv_part), "row")
    grad_ln1_gain, grad_ln1_shift, grad_ln2_gain, grad_ln2_shift = lax.psum(
        (gain_one_part, shift_one_part, gain_two_part, shift_two_part), "col"
    )
    return (
        block_output,
        grad_tokens,
        grad_ln1_gain,
        grad_ln1_shift,
        grad_weight_qkv,
        grad_bias_qkv,
        grad_weight_out,
        grad_bias_out,
        grad_ln2_gain,
        grad_ln2_shift,
        grad_weight_up,
        grad_bias_up,
        grad_weight_down,
        grad_bias_down,
    )


def solution(mesh):
    in_specs = (
        P("row", "col"),
        P("row"),
        P("row"),
        P("row", "col"),
        P("col"),
        P("row", "col"),
        P("row"),
        P("row"),
        P("row"),
        P("row", "col"),
        P("col"),
        P("row", "col"),
        P("row"),
        P("row", "col"),
    )
    out_specs = (
        P("row", "col"),
        P("row", "col"),
        P("row"),
        P("row"),
        P("row", "col"),
        P("col"),
        P("row", "col"),
        P("row"),
        P("row"),
        P("row"),
        P("row", "col"),
        P("col"),
        P("row", "col"),
        P("row"),
    )
    return jax.shard_map(body, mesh=mesh, in_specs=in_specs, out_specs=out_specs, check_vma=False)
```

profile of v0, /device:TPU:0, one launch (start us, length us, event | category | flops | bytes accessed | tf_op | source)
XLA Modules:
  0.0 4900.1 jit_solution(17613472183118926545)
XLA Ops:
  8.7 38.8 all-reduce.3
  50.7 26.6 all-gather.9.cloned.1.call-done
  94.8 625.4 %reduce-scatter.9.cloned.1.call-done = f32[1024,1200]{0,1:T(8,128)} async-done(((f32[8192,1200]{0,1:T(8,128)}), f32[1024,1200]{0,1:T(8,128)}) %reduce-scatter.9.cloned.1.call-update) | async-done | bytes 4915216 | tf_op jit(solution)/shard_map/reduce_scatter | solution.py:47
  733.7 18.4 reshape.182
  777.7 32.6 all-to-all-done
  818.2 51.8 %while.24 = (s32[]{:T(128)}, bf16[7,1024,64]{1,2,0:T(8,128)(2,1)S(1)}, f32[7,1024]{1,0:T(8,128)S(1)}, bf16[7,1024,192]{2,1,0:T(8,128)(2,1)}, s32[]{:T(128)}, /*index=5*/s32[]{:T(128)}) while((s32[]{:T(128)}, bf16[7,1024,64]{1,2,0:T(8,128)(2,1)S(1)}, f32[7,1024]{1,0:T(8,128)S(1)}, bf16[7,1024,192]{2,1,0:T(8,128)(2,1)}, s32[]{:T(128)}, ...), condition=%wide.region_8.9_spmd.clone, body=%wide.region_5.8_spmd.clone.sunk | while | flops 284228608 | bytes 30974060 | solution.py:170
  925.0 100.2 %all-gather.11.cloned.1.call-done = bf16[8192,400]{0,1:T(8,128)(2,1)} async-done(((bf16[1024,400]{0,1:T(8,128)(2,1)}), bf16[8192,400]{0,1:T(8,128)(2,1)}) %all-gather.11.cloned.1.call-update) | async-done | bytes 6553616 | tf_op jit(solution)/shard_map/all_gather | solution.py:69
  1033.3 57.8 %reduce-scatter.11.cloned.1.call-done = f32[200,2048]{1,0:T(8,128)} async-done(((f32[200,8192]{1,0:T(8,128)}), f32[200,2048]{1,0:T(8,128)}) %reduce-scatter.11.cloned.1.call-update) | async-done | bytes 1638416 | tf_op jit(solution)/shard_map/reduce_scatter | solution.py:62
  1093.0 37.1 all-reduce.2
  1131.5 22.0 fusion.71
  1157.1 22.8 fusion.70
  1180.2 802.1 %reduce-scatter.17.cloned.1.call-done = f32[1024,1600]{0,1:T(8,128)} async-done(((f32[8192,1600]{0,1:T(8,128)}), f32[1024,1600]{0,1:T(8,128)}) %reduce-scatter.17.cloned.1.call-update) | async-done | bytes 6553616 | tf_op jit(solution)/shard_map/reduce_scatter | solution.py:47
  1982.3 824.9 %reduce-scatter.13.cloned.1.call-done = f32[1024,1600]{0,1:T(8,128)} async-done(((f32[8192,1600]{0,1:T(8,128)}), f32[1024,1600]{0,1:T(8,128)}) %reduce-scatter.13.cloned.1.call-update) | async-done | bytes 6553616 | tf_op jit(solution)/shard_map/reduce_scatter | solution.py:47
  2818.1 499.3 %all-gather.19.cloned.1.call-done = bf16[8192,1600]{0,1:T(8,128)(2,1)} async-done(((bf16[1024,1600]{0,1:T(8,128)(2,1)}), bf16[8192,1600]{0,1:T(8,128)(2,1)}) %all-gather.19.cloned.1.call-update) | async-done | bytes 26214416 | tf_op jit(solution)/shard_map/all_gather | solution.py:89
  3330.8 60.2 %reduce-scatter.19.cloned.1.call-done = f32[200,2048]{1,0:T(8,128)} async-done(((f32[200,8192]{1,0:T(8,128)}), f32[200,2048]{1,0:T(8,128)}) %reduce-scatter.19.cloned.1.call-update) | async-done | bytes 1638416 | tf_op jit(solution)/shard_map/reduce_scatter | solution.py:62
  3393.8 37.1 all-reduce.1
  3434.1 25.5 all-gather.21.cloned.1.call-done
  3468.2 215.1 %reduce-scatter.21.cloned.1.call-done = f32[1024,400]{0,1:T(8,128)} async-done(((f32[8192,400]{0,1:T(8,128)}), f32[1024,400]{0,1:T(8,128)}) %reduce-scatter.21.cloned.1.call-update) | async-done | bytes 1638416 | tf_op jit(solution)/shard_map/reduce_scatter | solution.py:47
  3737.8 49.8 %while.25 = (s32[]{:T(128)}, bf16[7,1024,192]{1,2,0:T(8,128)(2,1)}, bf16[7,1024,192]{2,1,0:T(8,128)(2,1)}, f32[7,1024]{1,0:T(8,128)S(1)}, bf16[7,1024,64]{1,2,0:T(8,128)(2,1)S(1)}, /*index=5*/s32[]{:T(128)}) while((s32[]{:T(128)}, bf16[7,1024,192]{1,2,0:T(8,128)(2,1)}, bf16[7,1024,192]{2,1,0:T(8,128)(2,1)}, ...), condition=%wide.region_25.26_spmd.clone, body=%wide.region_23.25_spmd.clone.sunk | while | flops 683080704 | bytes 34886228 | solution.py:210
  3790.9 40.7 all_to_all.61
  3839.9 18.5 reshape.190
  3886.1 374.8 %all-gather.23.cloned.1.call-done = bf16[8192,1200]{0,1:T(8,128)(2,1)} async-done(((bf16[1024,1200]{0,1:T(8,128)(2,1)}), bf16[8192,1200]{0,1:T(8,128)(2,1)}) %all-gather.23.cloned.1.call-update) | async-done | bytes 19660816 | tf_op jit(solution)/shard_map/all_gather | solution.py:89
  4274.7 487.6 %all-gather.15.cloned.1.call-done = bf16[8192,1600]{0,1:T(8,128)(2,1)} async-done(((bf16[1024,1600]{0,1:T(8,128)(2,1)}), bf16[8192,1600]{0,1:T(8,128)(2,1)}) %all-gather.15.cloned.1.call-update) | async-done | bytes 26214416 | tf_op jit(solution)/shard_map/all_gather | solution.py:69
  4844.0 37.1 all-reduce
  (302 shorter events, 479.9 us)
Async XLA Ops:
  7.2 1149.9 %copy-start = (bf16[200,1600]{1,0:T(8,128)(2,1)S(1)}, bf16[200,1600]{1,0:T(8,128)(2,1)}, u32[]{:S(2)}) copy-start(bf16[200,1600]{1,0:T(8,128)(2,1)} %param.27) | copy-start | bytes 1920004
  7.2 70.1 %all-gather.9.cloned.1.call-start = ((), (), s32[]{:S(2)}) async-start(), calls=%async_computation.12 | async-start | bytes 4096000 | tf_op jit(solution)/shard_map/all_gather | solution.py:43
  50.6 669.6 %reduce-scatter.9.cloned.1.call-start = ((), (), s32[]{:S(2)}) async-start(), calls=%async_computation.13 | async-start | bytes 44236800 | tf_op jit(solution)/shard_map/reduce_scatter | solution.py:47
  94.7 625.5 %copy-start.31 = (f32[1200]{0:T(1024)S(1)}, f32[1200]{0:T(1024)}, u32[]{:S(2)}) copy-start(f32[1200]{0:T(1024)} %param.22) | copy-start | bytes 14404
  773.7 36.6 all-to-all-start
  777.6 247.6 %all-gather.11.cloned.1.call-start = ((), (), s32[]{:S(2)}) async-start(), calls=%async_computation.14 | async-start | bytes 7372800 | tf_op jit(solution)/shard_map/all_gather | solution.py:69
  924.5 166.6 %reduce-scatter.11.cloned.1.call-start = ((), (), s32[]{:S(2)}) async-start(), calls=%async_computation.15 | async-start | bytes 8192000 | tf_op jit(solution)/shard_map/reduce_scatter | solution.py:62
  1032.7 98.8 %all-gather.17.cloned.1.call-start = ((), (), s32[]{:S(2)}) async-start(), calls=%async_computation.20 | async-start | bytes 4096000 | tf_op jit(solution)/shard_map/all_gather | solution.py:43
  1033.3 123.8 %all-gather.13.cloned.1.call-start = ((), (), s32[]{:S(2)}) async-start(), calls=%async_computation.16 | async-start | bytes 4096000 | tf_op jit(solution)/shard_map/all_gather | solution.py:43
  1092.9 2337.9 %copy-start.3 = (f32[200,2048]{1,0:T(8,128)}, f32[200,2048]{1,0:T(8,128)S(1)}, u32[]{:S(2)}) copy-start(f32[200,2048]{1,0:T(8,128)S(1)} %get-tuple-element.163) | copy-start | bytes 4915204
  1130.1 2300.8 %copy-start.14 = (f32[2048]{0:T(1024)}, f32[2048]{0:T(1024)S(1)}, u32[]{:S(2)}) copy-start(f32[2048]{0:T(1024)S(1)} %get-tuple-element.171) | copy-start | bytes 24580
  1130.1 2300.8 %copy-start.16 = (f32[2048]{0:T(1024)}, f32[2048]{0:T(1024)S(1)}, u32[]{:S(2)}) copy-start(f32[2048]{0:T(1024)S(1)} %get-tuple-element.172) | copy-start | bytes 24580
  1131.4 851.0 %reduce-scatter.17.cloned.1.call-start = ((), (), s32[]{:S(2)}) async-start(), calls=%async_computation.21 | async-start | bytes 58982400 | tf_op jit(solution)/shard_map/reduce_scatter | solution.py:47
  1153.5 1653.8 %reduce-scatter.13.cloned.1.call-start = ((), (), s32[]{:S(2)}) async-start(), calls=%async_computation.17 | async-start | bytes 58982400 | tf_op jit(solution)/shard_map/reduce_scatter | solution.py:47
  1179.9 1627.3 %copy-start.30 = (f32[1600]{0:T(1024)S(1)}, f32[1600]{0:T(1024)}, u32[]{:S(2)}) copy-start(f32[1600]{0:T(1024)} %param.28) | copy-start | bytes 19204
  1180.0 2137.4 %all-gather.19.cloned.1.call-start = ((), (), s32[]{:S(2)}) async-start(), calls=%async_computation.22 | async-start | bytes 29491200 | tf_op jit(solution)/shard_map/all_gather | solution.py:89
  2818.0 572.9 %reduce-scatter.19.cloned.1.call-start = ((), (), s32[]{:S(2)}) async-start(), calls=%async_computation.23 | async-start | bytes 8192000 | tf_op jit(solution)/shard_map/reduce_scatter | solution.py:62
  3330.7 128.9 %all-gather.21.cloned.1.call-start = ((), (), s32[]{:S(2)}) async-start(), calls=%async_computation.24 | async-start | bytes 4096000 | tf_op jit(solution)/shard_map/all_gather | solution.py:43
  3433.9 249.4 %reduce-scatter.21.cloned.1.call-start = ((), (), s32[]{:S(2)}) async-start(), calls=%async_computation.25 | async-start | bytes 14745600 | tf_op jit(solution)/shard_map/reduce_scatter | solution.py:47
  3721.2 16.5 all-to-all-start.2
  3724.7 536.1 %all-gather.23.cloned.1.call-start = ((), (), s32[]{:S(2)}) async-start(), calls=%async_computation.26 | async-start | bytes 22118400 | tf_op jit(solution)/shard_map/all_gather | solution.py:89
  3885.3 877.1 %all-gather.15.cloned.1.call-start = ((), (), s32[]{:S(2)}) async-start(), calls=%async_computation.18 | async-start | bytes 29491200 | tf_op jit(solution)/shard_map/all_gather | solution.py:69
  3885.8 948.5 %reduce-scatter.23.cloned.1.call-start = ((), (), s32[]{:S(2)}) async-start(), calls=%async_computation.27 | async-start | bytes 8192000 | tf_op jit(solution)/shard_map/reduce_scatter | solution.py:62
  4274.7 612.9 %reduce-scatter.15.cloned.1.call-start = ((), (), s32[]{:S(2)}) async-start(), calls=%async_computation.19 | async-start | bytes 8192000 | tf_op jit(solution)/shard_map/reduce_scatter | solution.py:62
  (39 other events, 2126.2 us)
Sparse Core Ops, SparseCore 0:
  50.7 26.5 all-gather.8
  94.8 625.3 reduce-scatter.8
  924.6 100.4 all-gather.10
  1032.8 58.2 reduce-scatter.10
  1092.5 29.2 all-gather.16
  1131.5 25.5 all-gather.12
  1161.1 821.2 reduce-scatter.16
  1986.8 820.4 reduce-scatter.12
  2818.1 499.2 all-gather.18
  3330.8 60.0 reduce-scatter.18
  3434.0 25.5 all-gather.20
  3468.3 214.9 reduce-scatter.20
  3885.4 375.3 all-gather.22
  4262.3 500.0 all-gather.14
  4764.9 60.0 reduce-scatter.22
  4827.4 60.1 reduce-scatter.14
where the time goes:
time: 4910 us; the launch traced here: 4900 us
  waiting for transfers between devices  4160 us (85%)
  matrix products  234 us (5%)
  blocking collectives  215 us (4%)
  local copies, waits for them, and re-layouts  210 us (4%)
  other arithmetic  61.1 us (1%)
    reduce_scatter x4, waiting for transfers between devices, row_terms(): lax.psum_scatter(lax.dot_general(gathered, weight, (((0,), (0,)), ((), ()...  2470 us
    all_gather x2, waiting for transfers between devices, fold_rows(): lax.all_gather(gradient, 'row', axis=0, tiled=True)  874 us
    all_gather x2, waiting for transfers between devices, cross_products(): lax.all_gather(values, 'row', axis=0, tiled=True)  588 us
    psum x4, blocking collectives, row_totals(): return lax.psum((first_sum, second_sum), 'row')  150 us
    reduce_scatter x4, waiting for transfers between devices, share_cols(): return lax.psum_scatter(full_cols, 'col', scatter_dimension=1, tiled=True)  124 us
  transfers between devices with their start and end apart: 18, of which 16 were waited for; matrix products, arithmetic and copies ran while one was open for 3% of the time, Pallas kernels for 0%

commit v1 on v0

--- a/solution.py
+++ b/solution.py
@@ -10,6 +10,19 @@
 SEQ_ROW = 1
 epsilon = 1e-05
 excluded = -1e30
+
+
+def derive_loads(q_in):
+    o_now, local_out, block_last = (lax.axis_size("row"), lax.axis_index("row"), q_in.shape[0])
+    chunks = [(dev_j, (dev_j + 1) % o_now) for dev_j in range(o_now)]
+    y = jnp.zeros((*q_in.shape[:0], o_now * block_last, *q_in.shape[1:]), q_in.dtype)
+    y_new = q_in
+    for pp in range(o_now):
+        wide_out = (local_out - pp) % o_now
+        y = lax.dynamic_update_slice_in_dim(y, y_new, wide_out * block_last, axis=0)
+        if pp < o_now - 1:
+            y_new = lax.ppermute(y_new, axis_name="row", perm=chunks)
+    return y
 
 
 def row_totals(first_sum, second_sum):
@@ -66,7 +79,7 @@
     return share_cols(
         lax.dot_general(
             weight,
-            lax.all_gather(values, "row", axis=0, tiled=True),
+            derive_loads(values),
             (((1,), (1,)), ((), ())),
             preferred_element_type=jnp.float32,
         )

time: 4910 us -> 5590 us (1.14)
  waiting for transfers between devices: 4160 us -> 4790 us
    ppermute x0 -> x14, waiting for transfers between devices: none -> 698 us  [derive_loads(): y_new = lax.ppermute(y_new, axis_name='row', perm=chunks)]
    all_gather x2, waiting for transfers between devices: 588 us -> 503 us  [fold_again(): lax.all_gather(values, 'row', axis=0, tiled=True)]
  transfers between devices with their start and end apart: 18 -> 32, of which waited for: 16 -> 30; matrix products, arithmetic and copies ran while one was open for 3% -> 3% of each run, Pallas kernels for 0% -> 0%
where the time goes in v1:
time: 5590 us; the launch traced here: 5570 us
  waiting for transfers between devices  4790 us (86%)
  local copies, waits for them, and re-layouts  233 us (4%)
  blocking collectives  215 us (4%)
  matrix products  215 us (4%)
  other arithmetic  69.2 us (1%)
    reduce_scatter x4, waiting for transfers between devices, row_terms(): lax.psum_scatter(lax.dot_general(gathered, weight, (((0,), (0,)), ((), ()...  2470 us
    all_gather x2, waiting for transfers between devices, fold_rows(): lax.all_gather(gradient, 'row', axis=0, tiled=True)  849 us
    ppermute x14, waiting for transfers between devices, derive_loads(): y_new = lax.ppermute(y_new, axis_name='row', perm=chunks)  698 us
    all_gather x2, waiting for transfers between devices, fold_again(): lax.all_gather(values, 'row', axis=0, tiled=True)  503 us
    reduce_scatter x4, waiting for transfers between devices, share_cols(): return lax.psum_scatter(full_cols, 'col', scatter_dimension=1, tiled=True)  172 us
    psum x4, blocking collectives, row_totals(): return lax.psum((first_sum, second_sum), 'row')  151 us
  transfers between devices with their start and end apart: 32, of which 30 were waited for; matrix products, arithmetic and copies ran while one was open for 3% of the time, Pallas kernels for 0%

profile of v1, /device:TPU:0, one launch (start us, length us, event | category | flops | bytes accessed | tf_op | source)
XLA Modules:
  0.0 5574.5 jit_solution(8702668828624583694)
XLA Ops:
  8.7 38.8 all-reduce.3
  94.2 625.6 %reduce-scatter.9.cloned.1.call-done = f32[1024,1200]{0,1:T(8,128)} async-done(((f32[8192,1200]{0,1:T(8,128)}), f32[1024,1200]{0,1:T(8,128)}) %reduce-scatter.9.cloned.1.call-update) | async-done | bytes 4915216 | tf_op jit(solution)/shard_map/reduce_scatter | solution.py:60
  777.4 32.6 all-to-all-done
  1039.5 59.0 %reduce-scatter.11.cloned.1.call-done = f32[200,2048]{1,0:T(8,128)} async-done(((f32[200,8192]{1,0:T(8,128)}), f32[200,2048]{1,0:T(8,128)}) %reduce-scatter.11.cloned.1.call-update) | async-done | bytes 1638416 | tf_op jit(solution)/shard_map/reduce_scatter | solution.py:75
  1100.4 37.1 all-reduce.2
  1187.6 801.8 %reduce-scatter.17.cloned.1.call-done = f32[1024,1600]{0,1:T(8,128)} async-done(((f32[8192,1600]{0,1:T(8,128)}), f32[1024,1600]{0,1:T(8,128)}) %reduce-scatter.17.cloned.1.call-update) | async-done | bytes 6553616 | tf_op jit(solution)/shard_map/reduce_scatter | solution.py:60
  1989.5 824.9 %reduce-scatter.13.cloned.1.call-done = f32[1024,1600]{0,1:T(8,128)} async-done(((f32[8192,1600]{0,1:T(8,128)}), f32[1024,1600]{0,1:T(8,128)}) %reduce-scatter.13.cloned.1.call-update) | async-done | bytes 6553616 | tf_op jit(solution)/shard_map/reduce_scatter | solution.py:60
  2824.5 499.3 %all-gather.15.cloned.1.call-done = bf16[8192,1600]{0,1:T(8,128)(2,1)} async-done(((bf16[1024,1600]{0,1:T(8,128)(2,1)}), bf16[8192,1600]{0,1:T(8,128)(2,1)}) %all-gather.15.cloned.1.call-update) | async-done | bytes 26214416 | tf_op jit(solution)/shard_map/all_gather | solution.py:102
  3337.3 60.2 %reduce-scatter.19.cloned.1.call-done = f32[200,2048]{1,0:T(8,128)} async-done(((f32[200,8192]{1,0:T(8,128)}), f32[200,2048]{1,0:T(8,128)}) %reduce-scatter.19.cloned.1.call-update) | async-done | bytes 1638416 | tf_op jit(solution)/shard_map/reduce_scatter | solution.py:75
  3400.3 37.1 all-reduce.1
  3474.7 215.1 %reduce-scatter.21.cloned.1.call-done = f32[1024,400]{0,1:T(8,128)} async-done(((f32[8192,400]{0,1:T(8,128)}), f32[1024,400]{0,1:T(8,128)}) %reduce-scatter.21.cloned.1.call-update) | async-done | bytes 1638416 | tf_op jit(solution)/shard_map/reduce_scatter | solution.py:60
  3744.6 49.9 while.25
  3797.8 40.7 all_to_all.61
  3909.2 121.7 %collective-permute-done.7 = bf16[1024,1600]{0,1:T(8,128)(2,1)} collective-permute-done((bf16[1024,1600]{0,1:T(8,128)(2,1)}, bf16[1024,1600]{0,1:T(8,128)(2,1)}, u32[]{:S(2)}, u32[]{:S(2)}) %collective-permute-start.7) | collective-permute-done | bytes 3276832 | tf_op jit(solution)/shard_map/ppermute | solution.py:24
  4030.9 93.6 %collective-permute-done.8 = bf16[1024,1600]{0,1:T(8,128)(2,1)S(1)} collective-permute-done((bf16[1024,1600]{0,1:T(8,128)(2,1)}, bf16[1024,1600]{0,1:T(8,128)(2,1)S(1)}, u32[]{:S(2)}, u32[]{:S(2)}) %collective-permute-start.8) | collective-permute-done | bytes 3276832 | tf_op jit(solution)/shard_map/ppermute | solution.py:24
  4128.7 74.6 %collective-permute-done.9 = bf16[1024,1600]{0,1:T(8,128)(2,1)} collective-permute-done((bf16[1024,1600]{0,1:T(8,128)(2,1)S(1)}, bf16[1024,1600]{0,1:T(8,128)(2,1)}, u32[]{:S(2)}, u32[]{:S(2)}) %collective-permute-start.9) | collective-permute-done | bytes 3276832 | tf_op jit(solution)/shard_map/ppermute | solution.py:24
  4219.3 349.2 %all-gather.19.cloned.1.call-done = bf16[8192,1200]{0,1:T(8,128)(2,1)} async-done(((bf16[1024,1200]{0,1:T(8,128)(2,1)}), bf16[8192,1200]{0,1:T(8,128)(2,1)}) %all-gather.19.cloned.1.call-update) | async-done | bytes 19660816 | tf_op jit(solution)/shard_map/all_gather | solution.py:102
  4585.4 146.5 %collective-permute-done.11 = bf16[1024,1600]{0,1:T(8,128)(2,1)S(1)} collective-permute-done((bf16[1024,1600]{0,1:T(8,128)(2,1)}, bf16[1024,1600]{0,1:T(8,128)(2,1)S(1)}, u32[]{:S(2)}, u32[]{:S(2)}) %collective-permute-start.11) | collective-permute-done | bytes 3276832 | tf_op jit(solution)/shard_map/ppermute | solution.py:24
  4734.4 73.4 %collective-permute-done.12 = bf16[1024,1600]{0,1:T(8,128)(2,1)S(1)} collective-permute-done((bf16[1024,1600]{0,1:T(8,128)(2,1)S(1)}, bf16[1024,1600]{0,1:T(8,128)(2,1)S(1)}, u32[]{:S(2)}, u32[]{:S(2)}) %collective-permute-start.12) | collective-permute-done | bytes 3276832 | tf_op jit(solution)/shard_map/ppermute | solution.py:24
  4825.8 56.7 %collective-permute-done.13 = bf16[1024,1600]{0,1:T(8,128)(2,1)S(1)} collective-permute-done((bf16[1024,1600]{0,1:T(8,128)(2,1)S(1)}, bf16[1024,1600]{0,1:T(8,128)(2,1)S(1)}, u32[]{:S(2)}, u32[]{:S(2)}) %collective-permute-start.13) | collective-permute-done | bytes 3276832 | tf_op jit(solution)/shard_map/ppermute | solution.py:24
  4901.4 430.6 %all-gather.23.cloned.1.call-done = bf16[8192,1600]{0,1:T(8,128)(2,1)} async-done(((bf16[1024,1600]{0,1:T(8,128)(2,1)}), bf16[8192,1600]{0,1:T(8,128)(2,1)}) %all-gather.23.cloned.1.call-update) | async-done | bytes 26214416 | tf_op jit(solution)/shard_map/all_gather | solution.py:111
  5365.8 72.7 %all-gather.21.cloned.1.call-done = bf16[8192,400]{0,1:T(8,128)(2,1)} async-done(((bf16[1024,400]{0,1:T(8,128)(2,1)}), bf16[8192,400]{0,1:T(8,128)(2,1)}) %all-gather.21.cloned.1.call-update) | async-done | bytes 6553616 | tf_op jit(solution)/shard_map/all_gather | solution.py:111
  5462.8 36.6 reduce-scatter.23.cloned.1.call-done
  5508.0 37.9 all-reduce
  (339 shorter events, 815.8 us)
Async XLA Ops:
  7.2 70.1 %all-gather.9.cloned.1.call-start = ((), (), s32[]{:S(2)}) async-start(), calls=%async_computation.12 | async-start | bytes 4096000 | tf_op jit(solution)/shard_map/all_gather | solution.py:56
  50.6 669.3 %reduce-scatter.9.cloned.1.call-start = ((), (), s32[]{:S(2)}) async-start(), calls=%async_computation.13 | async-start | bytes 44236800 | tf_op jit(solution)/shard_map/reduce_scatter | solution.py:60
  773.7 36.4 all-to-all-start
  777.3 321.2 %reduce-scatter.11.cloned.1.call-start = ((), (), s32[]{:S(2)}) async-start(), calls=%async_computation.14 | async-start | bytes 8192000 | tf_op jit(solution)/shard_map/reduce_scatter | solution.py:75
  1038.9 100.0 %all-gather.13.cloned.1.call-start = ((), (), s32[]{:S(2)}) async-start(), calls=%async_computation.18 | async-start | bytes 4096000 | tf_op jit(solution)/shard_map/all_gather | solution.py:56
  1039.5 125.1 %all-gather.11.cloned.1.call-start = ((), (), s32[]{:S(2)}) async-start(), calls=%async_computation.15 | async-start | bytes 4096000 | tf_op jit(solution)/shard_map/all_gather | solution.py:56
  1138.8 850.6 %reduce-scatter.17.cloned.1.call-start = ((), (), s32[]{:S(2)}) async-start(), calls=%async_computation.19 | async-start | bytes 58982400 | tf_op jit(solution)/shard_map/reduce_scatter | solution.py:60
  1160.9 1653.5 %reduce-scatter.13.cloned.1.call-start = ((), (), s32[]{:S(2)}) async-start(), calls=%async_computation.16 | async-start | bytes 58982400 | tf_op jit(solution)/shard_map/reduce_scatter | solution.py:60
  1187.4 2136.4 %all-gather.15.cloned.1.call-start = ((), (), s32[]{:S(2)}) async-start(), calls=%async_computation.20 | async-start | bytes 29491200 | tf_op jit(solution)/shard_map/all_gather | solution.py:102
  2824.5 573.0 %reduce-scatter.19.cloned.1.call-start = ((), (), s32[]{:S(2)}) async-start(), calls=%async_computation.21 | async-start | bytes 8192000 | tf_op jit(solution)/shard_map/reduce_scatter | solution.py:75
  3337.2 128.9 %all-gather.17.cloned.1.call-start = ((), (), s32[]{:S(2)}) async-start(), calls=%async_computation.22 | async-start | bytes 4096000 | tf_op jit(solution)/shard_map/all_gather | solution.py:56
  3440.4 249.4 %reduce-scatter.21.cloned.1.call-start = ((), (), s32[]{:S(2)}) async-start(), calls=%async_computation.23 | async-start | bytes 14745600 | tf_op jit(solution)/shard_map/reduce_scatter | solution.py:60
  3731.5 837.1 %all-gather.19.cloned.1.call-start = ((), (), s32[]{:S(2)}) async-start(), calls=%async_computation.24 | async-start | bytes 22118400 | tf_op jit(solution)/shard_map/all_gather | solution.py:102
  3892.2 1439.8 %all-gather.23.cloned.1.call-start = ((), (), s32[]{:S(2)}) async-start(), calls=%async_computation.27 | async-start | bytes 29491200 | tf_op jit(solution)/shard_map/all_gather | solution.py:111
  3907.6 1531.0 %all-gather.21.cloned.1.call-start = ((), (), s32[]{:S(2)}) async-start(), calls=%async_computation.26 | async-start | bytes 7372800 | tf_op jit(solution)/shard_map/all_gather | solution.py:111
  3907.6 123.3 %collective-permute-start.7 = (bf16[1024,1600]{0,1:T(8,128)(2,1)}, bf16[1024,1600]{0,1:T(8,128)(2,1)}, u32[]{:S(2)}, u32[]{:S(2)}) collective-permute-start(bf16[1024,1600]{0,1:T(8,128)(2,1)} %get-tuple-element.164), channel_id=1, source_target_pairs={{0,4},{4,8},{8,12},{12,16},{16,20},{20,24},{24,28},{28,0},{1,5},{5... | collective-permute-start | bytes 9830408 | tf_op jit(solution)/shard_map/ppermute | solution.py:24
  3909.2 1590.2 %reduce-scatter.23.cloned.1.call-start = ((), (), s32[]{:S(2)}) async-start(), calls=%async_computation.25 | async-start | bytes 8192000 | tf_op jit(solution)/shard_map/reduce_scatter | solution.py:75
  4030.9 93.6 %collective-permute-start.8 = (bf16[1024,1600]{0,1:T(8,128)(2,1)}, bf16[1024,1600]{0,1:T(8,128)(2,1)S(1)}, u32[]{:S(2)}, u32[]{:S(2)}) collective-permute-start(bf16[1024,1600]{0,1:T(8,128)(2,1)} %collective-permute-done.7), channel_id=1, source_target_pairs={{0,4},{4,8},{8,12},{12,16},{16,20},{20,24},{24,28},{28,0},{1,5},{5... | collective-permute-start | bytes 9830408 | tf_op jit(solution)/shard_map/ppermute | solution.py:24
  4126.3 77.0 %collective-permute-start.9 = (bf16[1024,1600]{0,1:T(8,128)(2,1)S(1)}, bf16[1024,1600]{0,1:T(8,128)(2,1)}, u32[]{:S(2)}, u32[]{:S(2)}) collective-permute-start(bf16[1024,1600]{0,1:T(8,128)(2,1)S(1)} %collective-permute-done.8), channel_id=1, source_target_pairs={{0,4},{4,8},{8,12},{12,16},{16,20},{20,24},{24,28},{28,0},{1,5},{5... | collective-permute-start | bytes 9830408 | tf_op jit(solution)/shard_map/ppermute | solution.py:24
  4203.3 379.1 %collective-permute-start.10 = (bf16[1024,1600]{0,1:T(8,128)(2,1)}, bf16[1024,1600]{0,1:T(8,128)(2,1)}, u32[]{:S(2)}, u32[]{:S(2)}) collective-permute-start(bf16[1024,1600]{0,1:T(8,128)(2,1)} %collective-permute-done.9), channel_id=1, source_target_pairs={{0,4},{4,8},{8,12},{12,16},{16,20},{20,24},{24,28},{28,0},{1,5},{5... | collective-permute-start | bytes 9830408 | tf_op jit(solution)/shard_map/ppermute | solution.py:24
  4582.4 979.5 %reduce-scatter.15.cloned.1.call-start = ((), (), s32[]{:S(2)}) async-start(), calls=%async_computation.17 | async-start | bytes 8192000 | tf_op jit(solution)/shard_map/reduce_scatter | solution.py:75
  4582.4 149.5 %collective-permute-start.11 = (bf16[1024,1600]{0,1:T(8,128)(2,1)}, bf16[1024,1600]{0,1:T(8,128)(2,1)S(1)}, u32[]{:S(2)}, u32[]{:S(2)}) collective-permute-start(bf16[1024,1600]{0,1:T(8,128)(2,1)} %collective-permute-done.10), channel_id=1, source_target_pairs={{0,4},{4,8},{8,12},{12,16},{16,20},{20,24},{24,28},{28,0},{1,5},{5... | collective-permute-start | bytes 9830408 | tf_op jit(solution)/shard_map/ppermute | solution.py:24
  4732.0 75.7 %collective-permute-start.12 = (bf16[1024,1600]{0,1:T(8,128)(2,1)S(1)}, bf16[1024,1600]{0,1:T(8,128)(2,1)S(1)}, u32[]{:S(2)}, u32[]{:S(2)}) collective-permute-start(bf16[1024,1600]{0,1:T(8,128)(2,1)S(1)} %collective-permute-done.11), channel_id=1, source_target_pairs={{0,4},{4,8},{8,12},{12,16},{16,20},{20,24},{24,28},{28,0},{1,5},{5... | collective-permute-start | bytes 9830408 | tf_op jit(solution)/shard_map/ppermute | solution.py:24
  4807.7 74.8 %collective-permute-start.13 = (bf16[1024,1600]{0,1:T(8,128)(2,1)S(1)}, bf16[1024,1600]{0,1:T(8,128)(2,1)S(1)}, u32[]{:S(2)}, u32[]{:S(2)}) collective-permute-start(bf16[1024,1600]{0,1:T(8,128)(2,1)S(1)} %collective-permute-done.12), channel_id=1, source_target_pairs={{0,4},{4,8},{8,12},{12,16},{16,20},{20,24},{24,28},{28,0},{1,5},{5... | collective-permute-start | bytes 9830408 | tf_op jit(solution)/shard_map/ppermute | solution.py:24
  (49 other events, 13276.7 us)
Sparse Core Ops, SparseCore 0:
  50.7 26.5 all-gather.8
  94.2 625.5 reduce-scatter.8
  1039.0 59.4 reduce-scatter.10
  1099.9 29.2 all-gather.12
  1138.9 25.5 all-gather.10
  1168.3 821.0 reduce-scatter.16
  1993.9 820.4 reduce-scatter.12
  2824.6 499.2 all-gather.14
  3337.3 60.0 reduce-scatter.18
  3440.5 25.5 all-gather.16
  3474.8 214.9 reduce-scatter.20
  3892.3 676.2 all-gather.18
  4570.2 761.8 all-gather.22
  5334.3 104.1 all-gather.20
  5441.1 58.2 reduce-scatter.22
  5501.7 60.1 reduce-scatter.14
